TPU v7x, 512 devices: a whole 4x4x16 slice. The times are simulated.
512 devices in a mesh: occ: 64 (over z_lo, y, core), aux: 8 (over x, z_hi).
Axes of the slice: x: 4, y: 4, z: 16 (z_hi: 2, z_lo: 8; z = z_hi * 8 + z_lo), core: 2. Of those that a mesh axis runs over, the one named last changes fastest.
Arguments:
- half_blocks: bfloat16 [1536, 64, 6144], P('occ', None, 'aux'), may hold values from -0.796875 to 0.796875
- block_rows: int32 [64], replicated, may hold values from 1 to 24, 768 in all
- block_order: int32 [64], replicated, may hold values from 0 to 63, each once
- ao_to_virt: bfloat16 [768, 512], replicated, may hold values from -0.21875 to 0.21875
- occ_energy: float32 [64], replicated, may hold values from -2 to -0.5
- virt_energy: float32 [512], replicated, may hold values from 0.2 to 3
Outputs:
- gamma: float32 [64, 512, 6144], P('occ', None, 'aux')
Inputs may be any that keep to these rules, and one draw needn't show every extreme that they name: block_rows[s] is the number of AO functions held by device s of occ; the counts sum to 768 and one of them equals 24. A permutation; the runs of AO functions lie end to end in the order of block_order.
All inputs are finite; a program needn't handle non-finite values.
Results may differ from a plain program's by a relative error of at most 0.008.
Values may be sent and summed in bfloat16 or wider, within the bound.
No kernel may reach another device: no remote copies, remote signals or barrier semaphores. Data moves between devices by JAX's collectives and lax.ppermute only.
A program may use at most 64 MiB of HBM per device.

v0:
```python
import jax
import jax.numpy as jnp
from jax import lax
from jax.sharding import PartitionSpec as P

CYCLE = 3


def shifted(value, axis, by):
    devices = lax.axis_size(axis)
    return lax.ppermute(value, axis, [(i, (i + by) % devices) for i in range(devices)])


def ao_layout(block_rows, block_order, maxrows):
    device_count = block_rows.shape[0]
    matches = block_order[:, None] == jnp.arange(device_count, dtype=jnp.int32)[None, :]
    ordered = jnp.sum(jnp.where(matches, block_rows[None, :], 0), axis=1)
    before = jnp.cumsum(ordered) - ordered
    starts = jnp.sum(jnp.where(matches, before[:, None], 0), axis=0)
    offset = jnp.arange(maxrows, dtype=jnp.int32)
    in_block = offset[None, :] < block_rows[:, None]
    target = starts[:, None] + offset[None, :]
    return (in_block, target)


def build_table(block_rows, block_order, ao_to_virt, maxrows):
    in_block, target = ao_layout(block_rows, block_order, maxrows)
    row_index = jnp.where(in_block, target, 0).reshape(-1)
    ao_rows = jnp.take(ao_to_virt, row_index, axis=0)
    return jnp.where(in_block.reshape(-1, 1), ao_rows, jnp.zeros_like(ao_rows))


def contract_rows(ao_table, received):
    return lax.dot_general(
        ao_table, received, (((0,), (0,)), ((), ())), preferred_element_type=jnp.float32
    ).astype(jnp.bfloat16)


def shards(half_blocks, block_rows, block_order, ao_to_virt, occ_energy, virt_energy):
    maxrows = half_blocks.shape[0]
    device_count = occ_energy.shape[0]
    position = lax.axis_index("occ")
    ao_table = build_table(block_rows, block_order, ao_to_virt, maxrows)
    own_tile = contract_rows(
        ao_table,
        lax.all_to_all(half_blocks, "occ", split_axis=1, concat_axis=0, tiled=True)[:, 0, :],
    )
    density = jnp.zeros(own_tile.shape, jnp.float32)
    other_tile = own_tile
    for cycle_step in range(CYCLE + 1):
        if cycle_step > 0:
            other_tile = shifted(other_tile, "occ", 1)
        partner = (position - cycle_step) % device_count
        energy_gap = (
            virt_energy[:, None] + virt_energy[None, :] - occ_energy[position] - occ_energy[partner]
        )
        product = lax.dot_general(
            own_tile, other_tile, (((1,), (1,)), ((), ())), preferred_element_type=jnp.float32
        )
        partial_value = 2.0 * product - product.T
        merged = lax.psum(partial_value.astype(jnp.bfloat16), "aux").astype(jnp.float32)
        amplitudes = (merged / energy_gap).astype(jnp.bfloat16)
        density = density + jnp.dot(amplitudes, other_tile, preferred_element_type=jnp.float32)
    return density[None]


def solution(mesh):
    return jax.shard_map(
        shards,
        mesh=mesh,
        in_specs=(P("occ", None, "aux"), P(), P(), P(), P(), P()),
        out_specs=P("occ", None, "aux"),
        check_vma=False,
    )
```

profile of v0, /device:TPU:1, one launch (start us, length us, event | category | flops | bytes accessed | tf_op | source)
XLA Modules:
  0.0 594.4 jit_solution(5116064361449036951)
XLA Ops:
  6.5 4.4 copy.19
  11.0 17.5 %all-to-all-start = ((bf16[24,64,768]{2,0,1:T(8,128)(2,1)}), bf16[24,64,768]{2,0,1:T(8,128)(2,1)}, u32[]{:S(2)}, u32[]{:S(2)}) async-start(bf16[24,64,768]{2,0,1:T(8,128)(2,1)} %copy.19), calls=%async_computation | async-start | bytes 4718592 | tf_op jit(solution)/shard_map/all_to_all | solution.py:46
  29.7 4.8 gather_fusion
  34.5 100.6 %all-to-all-done = bf16[24,64,768]{2,0,1:T(8,128)(2,1)} async-done(((bf16[24,64,768]{2,0,1:T(8,128)(2,1)}), bf16[24,64,768]{2,0,1:T(8,128)(2,1)}, u32[]{:S(2)}, u32[]{:S(2)}) %all-to-all-start) | async-done | bytes 2359328 | tf_op jit(solution)/shard_map/all_to_all | solution.py:46
  135.1 3.4 fusion.5
  138.5 4.3 collective-permute-start
  142.8 8.9 %collective-permute-done = bf16[512,768]{1,0:T(8,128)(2,1)S(1)} collective-permute-done((bf16[512,768]{1,0:T(8,128)(2,1)S(1)}, bf16[512,768]{1,0:T(8,128)(2,1)S(1)}, u32[]{:S(2)}, u32[]{:S(2)}) %collective-permute-start) | collective-permute-done | bytes 786464 | tf_op jit(solution)/shard_map/ppermute | solution.py:11
  151.7 4.4 collective-permute-start.1
  156.7 1.3 copy.20
  158.0 2.3 fusion.11
  160.9 1.3 copy.21
  162.2 3.4 collective-permute-done.1
  165.6 4.0 collective-permute-start.2
  169.6 2.3 fusion.10
  171.9 1.7 fusion.39
  173.7 1.3 copy.22
  175.0 2.3 fusion.9
  177.2 10.5 %collective-permute-done.2 = bf16[512,768]{1,0:T(8,128)(2,1)S(1)} collective-permute-done((bf16[512,768]{1,0:T(8,128)(2,1)}, bf16[512,768]{1,0:T(8,128)(2,1)S(1)}, u32[]{:S(2)}, u32[]{:S(2)}) %collective-permute-start.2) | collective-permute-done | bytes 786464 | tf_op jit(solution)/shard_map/ppermute | solution.py:11
  189.7 2.3 fusion.8
  193.3 382.2 %all-reduce.3.cloned.1.call-done = (bf16[512,512]{0,1:T(8,128)(2,1)}, bf16[512,512]{0,1:T(8,128)(2,1)}, bf16[512,512]{0,1:T(8,128)(2,1)}, bf16[512,512]{0,1:T(8,128)(2,1)}) async-done(((bf16[512,512]{0,1:T(8,128)(2,1)}, bf16[512,512]{0,1:T(8,128)(2,1)}, bf16[512,512]{0,1:T(8,128)(2,1)}, bf16[512,512]{0,1:T(8,128)(2,1)}), (bf16[512,512]{0,1:T(8,128)(2,1)}, bf16[512,512]{0,1:T(8,128)(2,1)}, ...) | async-done | bytes 2097168 | tf_op jit(solution)/shard_map/psum | solution.py:61
  575.5 3.3 fusion.14
  578.8 2.2 fusion.15
  581.0 3.2 fusion.16
  584.2 3.3 add_bitcast_fusion
  (41 shorter events, 5.5 us)
Async XLA Ops:
  6.5 23.1 %copy-start = (bf16[768,512]{1,0:T(8,128)(2,1)S(1)}, bf16[768,512]{1,0:T(8,128)(2,1)}, u32[]{:S(2)}) copy-start(bf16[768,512]{1,0:T(8,128)(2,1)} %param.9) | copy-start | bytes 2359300
  11.0 17.6 %copy-start.6 = (s32[64]{0:T(128)S(1)}, s32[64]{0:T(128)}, u32[]{:S(2)}) copy-start(s32[64]{0:T(128)} %param.7) | copy-start | bytes 772
  11.0 17.6 %copy-start.9 = (s32[64]{0:T(128)S(1)}, s32[64]{0:T(128)}, u32[]{:S(2)}) copy-start(s32[64]{0:T(128)} %param.8) | copy-start | bytes 772
  11.0 124.2 %all-to-all-start = ((bf16[24,64,768]{2,0,1:T(8,128)(2,1)}), bf16[24,64,768]{2,0,1:T(8,128)(2,1)}, u32[]{:S(2)}, u32[]{:S(2)}) async-start(bf16[24,64,768]{2,0,1:T(8,128)(2,1)} %copy.19), calls=%async_computation | async-start | bytes 4718592 | tf_op jit(solution)/shard_map/all_to_all | solution.py:46
  28.5 547.0 %all-reduce.3.cloned.1.call-start = ((), (), s32[]{:S(2)}) async-start(), calls=%async_computation.1 | async-start | bytes 4194304 | tf_op jit(solution)/shard_map/psum | solution.py:61
  138.5 13.2 %collective-permute-start = (bf16[512,768]{1,0:T(8,128)(2,1)S(1)}, bf16[512,768]{1,0:T(8,128)(2,1)S(1)}, u32[]{:S(2)}, u32[]{:S(2)}) collective-permute-start(bf16[512,768]{1,0:T(8,128)(2,1)S(1)} %fusion.5), channel_id=1, source_target_pairs={{0,8},{8,16},{16,24},{24,32},{32,40},{40,48},{48,56},{56,64},{64,7... | collective-permute-start | bytes 2359304 | tf_op jit(solution)/shard_map/ppermute | solution.py:11
  151.7 8.6 %copy-start.1 = (bf16[512,768]{1,0:T(8,128)(2,1)}, bf16[512,768]{1,0:T(8,128)(2,1)S(1)}, u32[]{:S(2)}) copy-start(bf16[512,768]{1,0:T(8,128)(2,1)S(1)} %collective-permute-done) | copy-start | bytes 2359300
  151.7 13.9 %collective-permute-start.1 = (bf16[512,768]{1,0:T(8,128)(2,1)S(1)}, bf16[512,768]{1,0:T(8,128)(2,1)}, u32[]{:S(2)}, u32[]{:S(2)}) collective-permute-start(bf16[512,768]{1,0:T(8,128)(2,1)S(1)} %collective-permute-done), channel_id=1, source_target_pairs={{0,8},{8,16},{16,24},{24,32},{32,40},{40,48},{48,56},{56,64},{64,7... | collective-permute-start | bytes 2359304 | tf_op jit(solution)/shard_map/ppermute | solution.py:11
  165.6 22.2 %collective-permute-start.2 = (bf16[512,768]{1,0:T(8,128)(2,1)}, bf16[512,768]{1,0:T(8,128)(2,1)S(1)}, u32[]{:S(2)}, u32[]{:S(2)}) collective-permute-start(bf16[512,768]{1,0:T(8,128)(2,1)} %collective-permute-done.1), channel_id=1, source_target_pairs={{0,8},{8,16},{16,24},{24,32},{32,40},{40,48},{48,56},{56,64},{64,7... | collective-permute-start | bytes 2359304 | tf_op jit(solution)/shard_map/ppermute | solution.py:11
  192.0 0.7 copy-start.4
  192.0 383.5 %copy-start.5 = (f32[512]{0:T(512)S(1)}, f32[512]{0:T(512)}, u32[]{:S(2)}) copy-start(f32[512]{0:T(512)} %param.11) | copy-start | bytes 6148
  575.5 3.3 copy-start.2
  575.5 3.3 copy-start.8
  578.8 2.2 copy-start.7
  581.0 3.2 copy-start.3
Sparse Core Ops, SparseCore 0:
  192.1 383.2 all-reduce.2
where the time goes:
time: 595 us; the launch traced here: 594 us
  waiting for transfers between devices  506 us (85%)
  starting transfers between devices  30.2 us (5%)
  matrix products  18.9 us (3%)
  local copies, waits for them, and re-layouts  16.1 us (3%)
  between operations  13.7 us (2%)
  other arithmetic  9.85 us (2%)
    psum x1, waiting for transfers between devices, shards(): lax.psum(partial_value.astype(jnp.bfloat16), 'aux').astype(jnp.float32)  382 us
    all_to_all x1, waiting for transfers between devices, shards(): lax.all_to_all(half_blocks, 'occ', split_axis=1, concat_axis=0, tiled=True)  101 us
    ppermute x3, waiting for transfers between devices, shifted(): lax.ppermute(value, axis, [(i, (i + by) % devices) for i in range(devices)])  22.9 us
    all_to_all x1, starting transfers between devices, shards(): lax.all_to_all(half_blocks, 'occ', split_axis=1, concat_axis=0, tiled=True)  17.5 us
    ppermute x3, starting transfers between devices, shifted(): lax.ppermute(value, axis, [(i, (i + by) % devices) for i in range(devices)])  12.7 us
    dot_general x4, matrix products, shards(): jnp.dot(amplitudes, other_tile, preferred_element_type=jnp.float32)  12 us
  transfers between devices with their start and end apart: 5, of which 5 were waited for; matrix products, arithmetic and copies ran while one was open for 3% of the time, Pallas kernels for 0%

commit v1 on v0

--- a/solution.py
+++ b/solution.py
@@ -58,7 +58,9 @@
             own_tile, other_tile, (((1,), (1,)), ((), ())), preferred_element_type=jnp.float32
         )
         partial_value = 2.0 * product - product.T
-        merged = lax.psum(partial_value.astype(jnp.bfloat16), "aux").astype(jnp.float32)
+        merged = jnp.sum(lax.all_gather(partial_value.astype(jnp.bfloat16), "aux"), axis=0).astype(
+            jnp.float32
+        )
         amplitudes = (merged / energy_gap).astype(jnp.bfloat16)
         density = density + jnp.dot(amplitudes, other_tile, preferred_element_type=jnp.float32)
     return density[None]

time: 595 us -> 883 us (1.48)
  waiting for transfers between devices: 506 us -> 763 us
  local copies, waits for them, and re-layouts: 16.1 us -> 34.1 us
  other arithmetic: 9.85 us -> 22.8 us
    all_gather x0 -> x4, waiting for transfers between devices: none -> 615 us  [shards(): lax.all_gather(partial_value.astype(jnp.bfloat16), 'aux')]
    psum x1 -> x0, waiting for transfers between devices: 382 us -> none  [shards(): lax.psum(partial_value.astype(jnp.bfloat16), 'aux').astype(jnp.float32)]
    ppermute x3, waiting for transfers between devices: 22.9 us -> 47.1 us  [shifted(): lax.ppermute(value, axis, [(i, (i + by) % devices) for i in range(devices)])]
    unnamed x21 -> x29, local copies, waits for them, and re-layouts: 5.02 us -> 23.1 us
    reduce_sum x0 -> x4, other arithmetic: none -> 12.9 us  [shards(): jnp.sum(lax.all_gather(partial_value.astype(jnp.bfloat16), 'aux'), axis=0)]
  transfers between devices with their start and end apart: 5 -> 8, of which waited for: 5 -> 8; matrix products, arithmetic and copies ran while one was open for 3% -> 6% of each run, Pallas kernels for 0% -> 0%
where the time goes in v1:
time: 883 us; the launch traced here: 882 us
  waiting for transfers between devices  763 us (86%)
  local copies, waits for them, and re-layouts  34.1 us (4%)
  starting transfers between devices  30.3 us (3%)
  other arithmetic  22.8 us (3%)
  matrix products  18.4 us (2%)
  between operations  13.5 us (2%)
    all_gather x4, waiting for transfers between devices, shards(): lax.all_gather(partial_value.astype(jnp.bfloat16), 'aux')  615 us
    all_to_all x1, waiting for transfers between devices, shards(): lax.all_to_all(half_blocks, 'occ', split_axis=1, concat_axis=0, tiled=True)  101 us
    ppermute x3, waiting for transfers between devices, shifted(): lax.ppermute(value, axis, [(i, (i + by) % devices) for i in range(devices)])  47.1 us
    unnamed x29, local copies, waits for them, and re-layouts  23.1 us
  transfers between devices with their start and end apart: 8, of which 8 were waited for; matrix products, arithmetic and copies ran while one was open for 6% of the time, Pallas kernels for 0%

profile of v1, /device:TPU:1, one launch (start us, length us, event | category | flops | bytes accessed | tf_op | source)
XLA Modules:
  0.0 882.3 jit_solution(14704355480347619721)
XLA Ops:
  6.5 4.4 copy.25
  11.0 17.5 %all-to-all-start = ((bf16[24,64,768]{2,0,1:T(8,128)(2,1)}), bf16[24,64,768]{2,0,1:T(8,128)(2,1)}, u32[]{:S(2)}, u32[]{:S(2)}) async-start(bf16[24,64,768]{2,0,1:T(8,128)(2,1)} %copy.25), calls=%async_computation | async-start | bytes 4718592 | tf_op jit(solution)/shard_map/all_to_all | solution.py:46
  29.7 4.8 gather_fusion
  34.5 100.6 %all-to-all-done = bf16[24,64,768]{2,0,1:T(8,128)(2,1)} async-done(((bf16[24,64,768]{2,0,1:T(8,128)(2,1)}), bf16[24,64,768]{2,0,1:T(8,128)(2,1)}, u32[]{:S(2)}, u32[]{:S(2)}) %all-to-all-start) | async-done | bytes 2359328 | tf_op jit(solution)/shard_map/all_to_all | solution.py:46
  135.1 3.4 fusion.5
  142.7 4.3 collective-permute-start
  147.0 8.9 %collective-permute-done = bf16[512,768]{1,0:T(8,128)(2,1)S(1)} collective-permute-done((bf16[512,768]{1,0:T(8,128)(2,1)S(1)}, bf16[512,768]{1,0:T(8,128)(2,1)S(1)}, u32[]{:S(2)}, u32[]{:S(2)}) %collective-permute-start) | collective-permute-done | bytes 786464 | tf_op jit(solution)/shard_map/ppermute | solution.py:11
  160.3 4.4 collective-permute-start.1
  164.7 9.5 %collective-permute-done.1 = bf16[512,768]{1,0:T(8,128)(2,1)S(1)} collective-permute-done((bf16[512,768]{1,0:T(8,128)(2,1)S(1)}, bf16[512,768]{1,0:T(8,128)(2,1)S(1)}, u32[]{:S(2)}, u32[]{:S(2)}) %collective-permute-start.1) | collective-permute-done | bytes 786464 | tf_op jit(solution)/shard_map/ppermute | solution.py:11
  179.3 4.0 collective-permute-start.2
  183.3 28.7 %collective-permute-done.2 = bf16[512,768]{1,0:T(8,128)(2,1)S(1)} collective-permute-done((bf16[512,768]{1,0:T(8,128)(2,1)}, bf16[512,768]{1,0:T(8,128)(2,1)S(1)}, u32[]{:S(2)}, u32[]{:S(2)}) %collective-permute-start.2) | collective-permute-done | bytes 786464 | tf_op jit(solution)/shard_map/ppermute | solution.py:11
  217.0 107.4 %all-gather.9.cloned.1.call-done = bf16[4096,512]{0,1:T(8,128)(2,1)} async-done(((bf16[512,512]{0,1:T(8,128)(2,1)}), bf16[4096,512]{0,1:T(8,128)(2,1)}) %all-gather.9.cloned.1.call-update) | async-done | bytes 4194320 | tf_op jit(solution)/shard_map/all_gather | solution.py:61
  324.3 4.4 copy.30
  331.9 3.2 fusion.14
  335.1 174.7 %all-gather.11.cloned.1.call-done = bf16[4096,512]{0,1:T(8,128)(2,1)} async-done(((bf16[512,512]{0,1:T(8,128)(2,1)}), bf16[4096,512]{0,1:T(8,128)(2,1)}) %all-gather.11.cloned.1.call-update) | async-done | bytes 4194320 | tf_op jit(solution)/shard_map/all_gather | solution.py:61
  509.8 4.4 copy.31
  514.2 3.3 bitcast_reduce_fusion.2
  517.5 3.2 fusion.15
  520.8 166.7 %all-gather.13.cloned.1.call-done = bf16[4096,512]{0,1:T(8,128)(2,1)} async-done(((bf16[512,512]{0,1:T(8,128)(2,1)}), bf16[4096,512]{0,1:T(8,128)(2,1)}) %all-gather.13.cloned.1.call-update) | async-done | bytes 4194320 | tf_op jit(solution)/shard_map/all_gather | solution.py:61
  687.5 4.4 copy.32
  691.9 3.4 bitcast_reduce_fusion.1
  698.4 166.6 %all-gather.15.cloned.1.call-done = bf16[4096,512]{0,1:T(8,128)(2,1)} async-done(((bf16[512,512]{0,1:T(8,128)(2,1)}), bf16[4096,512]{0,1:T(8,128)(2,1)}) %all-gather.15.cloned.1.call-update) | async-done | bytes 4194320 | tf_op jit(solution)/shard_map/all_gather | solution.py:61
  865.1 4.4 copy.33
  872.7 3.1 add_bitcast_fusion
  (62 shorter events, 29.0 us)
Async XLA Ops:
  6.5 23.1 %copy-start = (bf16[768,512]{1,0:T(8,128)(2,1)S(1)}, bf16[768,512]{1,0:T(8,128)(2,1)}, u32[]{:S(2)}) copy-start(bf16[768,512]{1,0:T(8,128)(2,1)} %param.9) | copy-start | bytes 2359300
  11.0 17.6 %copy-start.10 = (s32[64]{0:T(128)S(1)}, s32[64]{0:T(128)}, u32[]{:S(2)}) copy-start(s32[64]{0:T(128)} %param.7) | copy-start | bytes 772
  11.0 17.6 %copy-start.11 = (s32[64]{0:T(128)S(1)}, s32[64]{0:T(128)}, u32[]{:S(2)}) copy-start(s32[64]{0:T(128)} %param.8) | copy-start | bytes 772
  11.0 124.2 %all-to-all-start = ((bf16[24,64,768]{2,0,1:T(8,128)(2,1)}), bf16[24,64,768]{2,0,1:T(8,128)(2,1)}, u32[]{:S(2)}, u32[]{:S(2)}) async-start(bf16[24,64,768]{2,0,1:T(8,128)(2,1)} %copy.25), calls=%async_computation | async-start | bytes 4718592 | tf_op jit(solution)/shard_map/all_to_all | solution.py:46
  28.5 295.8 %all-gather.9.cloned.1.call-start = ((), (), s32[]{:S(2)}) async-start(), calls=%async_computation.1 | async-start | bytes 4718592 | tf_op jit(solution)/shard_map/all_gather | solution.py:61
  142.7 367.1 %all-gather.11.cloned.1.call-start = ((), (), s32[]{:S(2)}) async-start(), calls=%async_computation.2 | async-start | bytes 4718592 | tf_op jit(solution)/shard_map/all_gather | solution.py:61
  142.7 13.2 %collective-permute-start = (bf16[512,768]{1,0:T(8,128)(2,1)S(1)}, bf16[512,768]{1,0:T(8,128)(2,1)S(1)}, u32[]{:S(2)}, u32[]{:S(2)}) collective-permute-start(bf16[512,768]{1,0:T(8,128)(2,1)S(1)} %fusion.5), channel_id=1, source_target_pairs={{0,8},{8,16},{16,24},{24,32},{32,40},{40,48},{48,56},{56,64},{64,7... | collective-permute-start | bytes 2359304 | tf_op jit(solution)/shard_map/ppermute | solution.py:11
  155.9 4.3 copy-start.4
  160.2 527.3 %all-gather.13.cloned.1.call-start = ((), (), s32[]{:S(2)}) async-start(), calls=%async_computation.3 | async-start | bytes 4718592 | tf_op jit(solution)/shard_map/all_gather | solution.py:61
  160.3 13.9 %collective-permute-start.1 = (bf16[512,768]{1,0:T(8,128)(2,1)S(1)}, bf16[512,768]{1,0:T(8,128)(2,1)S(1)}, u32[]{:S(2)}, u32[]{:S(2)}) collective-permute-start(bf16[512,768]{1,0:T(8,128)(2,1)S(1)} %collective-permute-done), channel_id=1, source_target_pairs={{0,8},{8,16},{16,24},{24,32},{32,40},{40,48},{48,56},{56,64},{64,7... | collective-permute-start | bytes 2359304 | tf_op jit(solution)/shard_map/ppermute | solution.py:11
  174.1 0.9 copy-start.6
  179.2 685.8 %all-gather.15.cloned.1.call-start = ((), (), s32[]{:S(2)}) async-start(), calls=%async_computation.4 | async-start | bytes 4718592 | tf_op jit(solution)/shard_map/all_gather | solution.py:61
  179.3 32.7 %collective-permute-start.2 = (bf16[512,768]{1,0:T(8,128)(2,1)}, bf16[512,768]{1,0:T(8,128)(2,1)S(1)}, u32[]{:S(2)}, u32[]{:S(2)}) collective-permute-start(bf16[512,768]{1,0:T(8,128)(2,1)} %copy-done.6), channel_id=1, source_target_pairs={{0,8},{8,16},{16,24},{24,32},{32,40},{40,48},{48,56},{56,64},{64,7... | collective-permute-start | bytes 2359304 | tf_op jit(solution)/shard_map/ppermute | solution.py:11
  213.9 2.4 copy-start.8
  328.7 3.1 copy-start.9
  514.2 3.3 copy-start.5
  691.9 3.4 copy-start.7
  869.5 3.2 copy-start.1
  869.5 3.2 copy-start.2
  869.5 3.2 copy-start.3
Sparse Core Ops, SparseCore 0:
  142.8 181.4 all-gather.8
  327.4 182.3 all-gather.10
  512.8 174.6 all-gather.12
  690.4 174.6 all-gather.14
